TPU v7x, 512 devices: a whole 4x4x16 slice. The times are simulated.
512 devices in a mesh: gx: 64 (over z, y), gy: 8 (over x, core).
Axes of the slice: x: 4, y: 4, z: 16, core: 2. Of those that a mesh axis runs over, the one named last changes fastest.
Arguments:
- velocity: float32 [3, 256, 64, 256], P(None, 'gx', 'gy'), may hold values from -6 to 6
- cotangent: float32 [3, 256, 64, 256], P(None, 'gx', 'gy'), may hold values from -10.5 to 13.5
- weight_in: float32 [6, 64], replicated, may hold values from -2.5 to 2.5
- bias_in: float32 [64], replicated, may hold values from -3 to 3
- weight_out: float32 [64, 3], replicated, may hold values from -0.75 to 0.75
Outputs:
- new_velocity: float32 [3, 256, 64, 256], P(None, 'gx', 'gy')
- grad_velocity: float32 [3, 256, 64, 256], P(None, 'gx', 'gy')
- grad_weight_in: float32 [6, 64], replicated
- grad_bias_in: float32 [64], replicated
- grad_weight_out: float32 [64, 3], replicated
All inputs are finite; a program needn't handle non-finite values.
Results may differ from a plain program's by a relative error of at most 0.0003.
Values sent between devices are 32-bit elements; how exact they have to be, the bound alone decides.
A program may use at most 64 MiB of HBM per device.

v0:
```python
import jax
import jax.numpy as jnp
import numpy as np
from jax import lax
from jax.sharding import PartitionSpec as P

FILTER_ALPHA = 0.499
FILTER_GAIN = 0.5 + FILTER_ALPHA
COMPACT_ALPHA = 1.0 / 3.0
STEP_SIZE = 0.5
PRECISE = lax.Precision.HIGHEST


def extended(array, sides, width):
    for axis, dim in sides:
        devices, length = (lax.axis_size(axis), array.shape[dim])
        up = [(i, (i + 1) % devices) for i in range(devices - 1)]
        down = [(j, i) for i, j in up]
        last = lax.slice_in_dim(array, length - width, length, axis=dim)
        leading = lax.slice_in_dim(array, 0, width, axis=dim)
        before = lax.ppermute(last, axis, up)
        after = lax.ppermute(leading, axis, down)
        array = jnp.concatenate([before, array, after], axis=dim)
    return array


def carried_in(part, axis, combine, identity, reverse):
    count = lax.axis_size(axis)
    place = lax.axis_index(axis)
    ahead = count - 1 - place if reverse else place
    gathered = jax.tree.map(lambda a: lax.all_gather(a, axis), part)
    state = jax.tree.map(lambda a, e: jnp.zeros_like(a) + jnp.asarray(e, a.dtype), part, identity)

    def one(turn, state):
        source = count - 1 - turn if reverse else turn
        return combine(
            state, jax.tree.map(lambda a: lax.dynamic_index_in_dim(a, source, 0, False), gathered)
        )

    return lax.fori_loop(0, ahead, one, state)


def derivative_table(length):
    weights = 7.0 / 9.0 * (np.eye(length, k=1) - np.eye(length, k=-1)) + 1.0 / 36.0 * (
        np.eye(length, k=2) - np.eye(length, k=-2)
    )
    uppers = np.zeros(length)
    before = 0.0
    previous = np.zeros(length)
    for position in range(length):
        scale = 1.0 / (1.0 - COMPACT_ALPHA * before)
        weights[position] = (weights[position] - COMPACT_ALPHA * previous) * scale
        before = COMPACT_ALPHA * scale
        uppers[position] = before
        previous = weights[position]
    for position in reversed(range(length - 1)):
        weights[position] = weights[position] - uppers[position] * weights[position + 1]
    return weights.astype(np.float32)


def sweep_tables(length):
    scales = np.zeros(length)
    uppers = np.zeros(length)
    before = 0.0
    for position in range(length):
        scales[position] = 1.0 / (1.0 - FILTER_ALPHA * before)
        before = FILTER_ALPHA * scales[position]
        uppers[position] = before
    return (scales.astype(np.float32), uppers.astype(np.float32))


def combine(earlier, later):
    return (earlier[0] * later[0], later[0] * earlier[1] + later[1])


def smooth_x(values):
    x_rows = values.shape[1]
    scales_all, uppers_all = sweep_tables(x_rows * lax.axis_size("gx"))
    offset = lax.axis_index("gx") * x_rows
    scales = lax.dynamic_slice_in_dim(jnp.asarray(scales_all), offset, x_rows)
    uppers = lax.dynamic_slice_in_dim(jnp.asarray(uppers_all), offset, x_rows)
    padded = extended(values, (("gx", 1),), 1)
    right_side = FILTER_GAIN * values + 0.5 * FILTER_GAIN * (padded[:, :-2] + padded[:, 2:])
    previous = jnp.zeros_like(values[:, 0])
    factor = jnp.ones((1, 1), jnp.float32)
    partial_rows = []
    factors = []
    for row_index in range(x_rows):
        previous = (right_side[:, row_index] - FILTER_ALPHA * previous) * scales[row_index]
        factor = factor * (-FILTER_ALPHA * scales[row_index])
        partial_rows.append(previous)
        factors.append(factor)
    identity = (jnp.ones((1, 1), jnp.float32), jnp.zeros_like(previous))
    incoming = carried_in((factor, previous), "gx", combine, identity, False)
    eliminated = [
        partial_rows[row_index] + factors[row_index] * incoming[1] for row_index in range(x_rows)
    ]
    following = jnp.zeros_like(previous)
    factor = jnp.ones((1, 1), jnp.float32)
    solved_rows = [None] * x_rows
    back_factors = [None] * x_rows
    for row_index in reversed(range(x_rows)):
        following = eliminated[row_index] - uppers[row_index] * following
        factor = factor * -uppers[row_index]
        solved_rows[row_index] = following
        back_factors[row_index] = factor
    upper_value = carried_in((factor, following), "gx", combine, identity, True)
    finished = [
        solved_rows[row_index] + back_factors[row_index] * upper_value[1]
        for row_index in range(x_rows)
    ]
    return jnp.stack(finished, axis=1)


def y_pass(values, table):
    derived = jnp.einsum(
        "ab,kxbz->kxaz",
        table,
        lax.all_to_all(values, "gy", split_axis=3, concat_axis=2, tiled=True),
        precision=PRECISE,
    )
    return lax.all_to_all(derived, "gy", split_axis=2, concat_axis=3, tiled=True)


def closure_plane(feature_plane, cotangent_plane, weight_in, bias_in, weight_out):
    pre = jnp.dot(weight_in.T, feature_plane, precision=PRECISE) + bias_in[:, None]
    hidden = jnp.tanh(pre)
    forcing = jnp.dot(weight_out.T, hidden, precision=PRECISE)
    grad_out = STEP_SIZE * cotangent_plane
    grad_hidden = jnp.dot(weight_out, grad_out, precision=PRECISE)
    grad_pre = grad_hidden * (1.0 - hidden * hidden)
    grad_feature = jnp.dot(weight_in, grad_pre, precision=PRECISE)
    sum_in = jnp.dot(feature_plane, grad_pre.T, precision=PRECISE)
    sum_bias = jnp.sum(grad_pre, axis=1)
    sum_out = jnp.dot(hidden, grad_out.T, precision=PRECISE)
    return (forcing, grad_feature, sum_in, sum_bias, sum_out)


def local(velocity, cotangent, weight_in, bias_in, weight_out):
    x_rows = velocity.shape[1]
    y_rows = velocity.shape[2]
    z_length = velocity.shape[3]
    y_length = y_rows * lax.axis_size("gy")
    y_table = jnp.asarray(derivative_table(y_length))
    z_table = jnp.asarray(derivative_table(z_length))
    smoothed = smooth_x(velocity)
    along_z = jnp.einsum("ab,kxyb->kxya", z_table, smoothed, precision=PRECISE)
    along_y = y_pass(smoothed, y_table)
    features = jnp.concatenate([along_y, along_z], axis=0)
    plane_cells = y_rows * z_length
    forcing_rows = []
    gradient_rows = []
    sum_in = jnp.zeros((6, weight_in.shape[1]), jnp.float32)
    sum_bias = jnp.zeros((weight_in.shape[1],), jnp.float32)
    sum_out = jnp.zeros((weight_in.shape[1], 3), jnp.float32)
    for row_index in range(x_rows):
        feature_plane = features[:, row_index].reshape(6, plane_cells)
        cotangent_plane = cotangent[:, row_index].reshape(3, plane_cells)
        forcing, grad_feature, part_in, part_bias, part_out = closure_plane(
            feature_plane, cotangent_plane, weight_in, bias_in, weight_out
        )
        forcing_rows.append(forcing.reshape(3, y_rows, z_length))
        gradient_rows.append(grad_feature.reshape(6, y_rows, z_length))
        sum_in = sum_in + part_in
        sum_bias = sum_bias + part_bias
        sum_out = sum_out + part_out
    new_velocity = velocity + STEP_SIZE * jnp.stack(forcing_rows, axis=1)
    grad_features = jnp.stack(gradient_rows, axis=1)
    back_y = y_pass(grad_features[0:3], y_table.T)
    back_z = jnp.einsum("ba,kxyb->kxya", z_table, grad_features[3:6], precision=PRECISE)
    grad_velocity = cotangent + smooth_x(back_y + back_z)
    totals = lax.psum((sum_in, sum_bias, sum_out), ("gx", "gy"))
    cells = float(x_rows * lax.axis_size("gx") * y_length * z_length)
    return (new_velocity, grad_velocity, totals[0] / cells, totals[1] / cells, totals[2] / cells)


def solution(mesh):
    in_specs = (P(None, "gx", "gy", None), P(None, "gx", "gy", None), P(), P(), P())
    out_specs = (P(None, "gx", "gy", None), P(None, "gx", "gy", None), P(), P(), P())
    return jax.shard_map(local, mesh=mesh, in_specs=in_specs, out_specs=out_specs, check_vma=False)
```

profile of v0, /device:TPU:2, one launch (start us, length us, event | category | flops | bytes accessed | tf_op | source)
XLA Modules:
  0.0 1216.4 jit_solution(16932506660493872590)
XLA Ops:
  8.0 3.5 collective-permute-start
  15.1 2.1 collective-permute-done.1
  17.2 3.0 multiply_bitcast_fusion.1
  30.8 149.0 %all-reduce.3 = (f32[64]{0:T(128)S(1)}, f32[64]{0:T(128)S(1)}) all-reduce(f32[64]{0:T(128)S(1)} %dynamic-update-slice.1, f32[64]{0:T(128)S(1)} %dynamic-update-slice), channel_id=1, replica_groups=mesh['gx'=64,'gy'=8] {'gx'}, use_global_device_ids=true, to_apply=%add.1 | all-reduce | flops 128 | bytes 1024
  179.9 4.9 fusion.30
  184.8 252.8 %all-gather.9.cloned.1.call-done = f32[192,8,256]{2,1,0:T(8,128)} async-done(((f32[3,8,256]{2,1,0:T(8,128)}), f32[192,8,256]{2,1,0:T(8,128)}) %all-gather.9.cloned.1.call-update) | async-done | bytes 1572880 | tf_op jit(solution)/shard_map/all_gather | solution.py:31
  437.6 124.3 %while.53 = (s32[]{:T(128)}, f32[3,8,256]{2,1,0:T(8,128)S(1)}, s32[]{:T(128)}, f32[64,1,1]{0,2,1:T(1,128)S(1)}, f32[64,3,8,256]{3,2,1,0:T(8,128)}, /*index=5*/s32[]{:T(128)}, s32[]{:T(128)}, s32[]{:T(128)}, s32[]{:T(128)}) while((s32[]{:T(128)}, f32[3,8,256]{2,1,0:T(8,128)S(1)}, s32[]{:T(128)}, f32[64,1,1]{0,2,1:T(1,128)S(1)}, ...), condition=%wide.region_3.4_spmd, body=%wide.region_2.3_spmd.sunk | while | flops 12294 | bytes 73895 | solution.py:40
  438.2 1.4 bitcast_add_fusion.11
  440.2 1.4 bitcast_add_fusion.11
  442.1 1.4 bitcast_add_fusion.11
  444.1 1.4 bitcast_add_fusion.11
  446.1 1.4 bitcast_add_fusion.11
  448.0 1.4 bitcast_add_fusion.11
  450.0 1.4 bitcast_add_fusion.11
  452.0 1.4 bitcast_add_fusion.11
  454.0 1.4 bitcast_add_fusion.11
  455.9 1.4 bitcast_add_fusion.11
  457.9 1.4 bitcast_add_fusion.11
  459.9 1.4 bitcast_add_fusion.11
  461.9 1.4 bitcast_add_fusion.11
  465.8 1.4 bitcast_add_fusion.11
  467.8 1.4 bitcast_add_fusion.11
  469.8 1.4 bitcast_add_fusion.11
  471.7 1.4 bitcast_add_fusion.11
  561.9 2.5 add_bitcast_fusion.6
  565.2 2.4 reshape.250
  567.6 4.8 all-to-all-start
  572.6 4.2 all-to-all-done
  578.2 1.9 reshape.251
  582.7 4.7 all-to-all-start.1
  587.8 4.0 all-to-all-done.1
  603.9 1.5 copy.85
  605.4 3.2 reshape.254
  608.6 8.2 all_to_all.72
  617.6 3.1 reshape.255
  620.7 2.2 copy.86
  623.9 2.2 convolution_bitcast_fusion
  628.2 9.1 all_to_all.73
  637.3 1.5 reduce.7
  644.9 4.2 collective-permute-done.3
  649.2 3.0 multiply_bitcast_fusion
  656.0 124.5 %all-gather.15.cloned.1.call-done = f32[192,1,8,256]{3,2,1,0:T(8,128)} async-done(((f32[3,1,8,256]{3,2,1,0:T(8,128)}), f32[192,1,8,256]{3,2,1,0:T(8,128)}) %all-gather.15.cloned.1.call-update) | async-done | bytes 1572880 | tf_op jit(solution)/shard_map/all_gather | solution.py:31
  780.6 4.9 fusion.24
  787.3 1.6 convolution_add_fusion.5
  788.9 262.2 %all-reduce.2 = (f32[6,64]{1,0:T(8,128)S(1)}, f32[64]{0:T(128)S(1)}, f32[64,3]{0,1:T(4,128)S(1)}) all-reduce(f32[6,64]{1,0:T(8,128)S(1)} %convolution_add_fusion.5, f32[64]{0:T(128)S(1)} %add_add_fusion, f32[64,3]{0,1:T(4,128)S(1)} %convolution_add_fusion.8), channel_id=1, replica_groups=mesh['gx'=64,'gy'=8] {'gx','gy'}, use_global_device_ids=true, to_apply=%region_8.9 | all-reduce | flops 640 | bytes 5120 | tf_op jit(solution)/shard_map/psum | solution.py:172
  1055.1 25.8 %all-gather.11.cloned.1.call-done = f32[192,8,256]{2,1,0:T(8,128)} async-done(((f32[3,8,256]{2,1,0:T(8,128)}), f32[192,8,256]{2,1,0:T(8,128)}) %all-gather.11.cloned.1.call-update) | async-done | bytes 1572880 | tf_op jit(solution)/shard_map/all_gather | solution.py:31
  1080.9 126.5 %while.55 = (s32[]{:T(128)}, f32[3,8,256]{2,1,0:T(8,128)S(1)}, s32[]{:T(128)}, f32[64,1,1]{0,2,1:T(1,128)S(1)}, f32[64,3,8,256]{3,2,1,0:T(8,128)}, /*index=5*/s32[]{:T(128)}, s32[]{:T(128)}, s32[]{:T(128)}, s32[]{:T(128)}) while((s32[]{:T(128)}, f32[3,8,256]{2,1,0:T(8,128)S(1)}, s32[]{:T(128)}, f32[64,1,1]{0,2,1:T(1,128)S(1)}, ...), condition=%wide.region_7.8_spmd, body=%wide.region_6.7_spmd.sunk | while | flops 12294 | bytes 73895 | solution.py:40
  1207.4 1.8 add_bitcast_fusion.2
  (399 shorter events, 273.0 us)
Async XLA Ops:
  7.2 586.2 %copy-start = (f32[6,64]{1,0:T(8,128)S(1)}, f32[6,64]{1,0:T(8,128)}, u32[]{:S(2)}) copy-start(f32[6,64]{1,0:T(8,128)} %param.21) | copy-start | bytes 4612
  7.2 172.6 %all-gather.13.cloned.1.call-start = ((), (), s32[]{:S(2)}) async-start(), calls=%async_computation.6 | async-start | bytes 1597440 | tf_op jit(solution)/shard_map/all_gather | solution.py:31
  8.0 7.1 collective-permute-start
  11.5 5.7 collective-permute-start.1
  20.3 417.3 %all-gather.9.cloned.1.call-start = ((), (), s32[]{:S(2)}) async-start(), calls=%async_computation.4 | async-start | bytes 1597440 | tf_op jit(solution)/shard_map/all_gather | solution.py:31
  179.9 257.7 %copy-start.29 = (f32[64,1,1]{0,2,1:T(1,128)}, f32[64,1,1]{0,2,1:T(1,128)S(1)}, u32[]{:S(2)}) copy-start(f32[64,1,1]{0,2,1:T(1,128)S(1)} %get-tuple-element.634) | copy-start | bytes 772
  561.9 2.5 copy-start.27
  564.4 8.0 copy-start.13
  567.6 9.2 all-to-all-start
  572.5 28.2 %copy-start.19 = (f32[1,3,8,256]{3,1,2,0:T(4,128)}, f32[1,3,8,256]{3,1,2,0:T(4,128)S(1)}, u32[]{:S(2)}) copy-start(f32[1,3,8,256]{3,1,2,0:T(4,128)S(1)} %copy.110) | copy-start | bytes 73732
  572.5 24.8 %copy-start.15 = (f32[1,3,8,256]{3,1,2,0:T(4,128)}, f32[1,3,8,256]{3,1,2,0:T(4,128)S(1)}, u32[]{:S(2)}) copy-start(f32[1,3,8,256]{3,1,2,0:T(4,128)S(1)} %copy.114) | copy-start | bytes 73732
  572.5 23.6 %copy-start.20 = (f32[1,3,8,256]{3,1,2,0:T(4,128)}, f32[1,3,8,256]{3,1,2,0:T(4,128)S(1)}, u32[]{:S(2)}) copy-start(f32[1,3,8,256]{3,1,2,0:T(4,128)S(1)} %copy.112) | copy-start | bytes 73732
  572.6 26.4 %copy-start.17 = (f32[1,3,8,256]{3,1,2,0:T(4,128)}, f32[1,3,8,256]{3,1,2,0:T(4,128)S(1)}, u32[]{:S(2)}) copy-start(f32[1,3,8,256]{3,1,2,0:T(4,128)S(1)} %copy.116) | copy-start | bytes 73732
  578.2 2.6 copy-start.25
  580.6 6.8 copy-start.22
  582.7 9.1 all-to-all-start.1
  587.4 193.2 %all-gather.15.cloned.1.call-start = ((), (), s32[]{:S(2)}) async-start(), calls=%async_computation.7 | async-start | bytes 1597440 | tf_op jit(solution)/shard_map/all_gather | solution.py:31
  592.9 0.7 copy-start.26
  593.2 2.9 copy-start.24
  593.3 2.9 copy-start.11
  593.3 2.2 copy-start.7
  593.3 2.8 copy-start.5
  593.4 2.1 copy-start.9
  600.2 3.7 copy-start.1
  602.0 0.8 copy-start.2
  640.8 13.1 %copy-start.21 = (f32[1,3,8,256]{3,1,2,0:T(4,128)S(1)}, f32[1,3,8,256]{3,1,2,0:T(4,128)}, u32[]{:S(2)}) copy-start(f32[1,3,8,256]{3,1,2,0:T(4,128)} %copy-done.20) | copy-start | bytes 73732
  640.8 13.6 %copy-start.16 = (f32[1,3,8,256]{3,1,2,0:T(4,128)S(1)}, f32[1,3,8,256]{3,1,2,0:T(4,128)}, u32[]{:S(2)}) copy-start(f32[1,3,8,256]{3,1,2,0:T(4,128)} %copy-done.15) | copy-start | bytes 73732
  640.8 14.7 %copy-start.12 = (f32[1,6,8,256]{3,1,2,0:T(8,128)S(1)}, f32[1,6,8,256]{3,1,2,0:T(8,128)}, u32[]{:S(2)}) copy-start(f32[1,6,8,256]{3,1,2,0:T(8,128)} %copy-done.11) | copy-start | bytes 147460
  642.1 2.8 collective-permute-start.2
  643.4 5.7 collective-permute-start.3
  652.2 428.6 %all-gather.11.cloned.1.call-start = ((), (), s32[]{:S(2)}) async-start(), calls=%async_computation.5 | async-start | bytes 1597440 | tf_op jit(solution)/shard_map/all_gather | solution.py:31
  652.5 2.4 copy-start.18
  652.5 3.0 copy-start.3
  653.9 132.4 %copy-start.8 = (f32[1,6,8,256]{3,1,2,0:T(8,128)S(1)}, f32[1,6,8,256]{3,1,2,0:T(8,128)}, u32[]{:S(2)}) copy-start(f32[1,6,8,256]{3,1,2,0:T(8,128)} %copy-done.7) | copy-start | bytes 147460
  654.4 132.3 %copy-start.10 = (f32[1,6,8,256]{3,1,2,0:T(8,128)S(1)}, f32[1,6,8,256]{3,1,2,0:T(8,128)}, u32[]{:S(2)}) copy-start(f32[1,6,8,256]{3,1,2,0:T(8,128)} %copy-done.9) | copy-start | bytes 147460
  655.0 132.3 %copy-start.6 = (f32[1,6,8,256]{3,1,2,0:T(8,128)S(1)}, f32[1,6,8,256]{3,1,2,0:T(8,128)}, u32[]{:S(2)}) copy-start(f32[1,6,8,256]{3,1,2,0:T(8,128)} %copy-done.5) | copy-start | bytes 147460
  787.3 267.1 %copy-start.4 = (f32[3,4,8,256]{3,2,1,0:T(8,128)S(1)}, f32[3,4,8,256]{3,2,1,0:T(8,128)}, u32[]{:S(2)}) copy-start(f32[3,4,8,256]{3,2,1,0:T(8,128)} %param.19) | copy-start | bytes 294916
  787.3 293.6 %copy-start.28 = (f32[64,1,1]{0,2,1:T(1,128)S(1)}, f32[64,1,1]{0,2,1:T(1,128)}, u32[]{:S(2)}) copy-start(f32[64,1,1]{0,2,1:T(1,128)} %copy-done.27) | copy-start | bytes 772
  1053.2 154.2 %copy-start.23 = (f32[3,8,256]{2,1,0:T(8,128)S(1)}, f32[3,8,256]{2,1,0:T(8,128)}, u32[]{:S(2)}) copy-start(f32[3,8,256]{2,1,0:T(8,128)} %get-tuple-element.325) | copy-start | bytes 73732
  1053.2 156.0 %copy-start.14 = (f32[3,4,8,256]{3,2,1,0:T(8,128)S(1)}, f32[3,4,8,256]{3,2,1,0:T(8,128)}, u32[]{:S(2)}) copy-start(f32[3,4,8,256]{3,2,1,0:T(8,128)} %param.20) | copy-start | bytes 294916
Sparse Core Ops, SparseCore 0:
  20.4 146.7 all-gather.12
  185.0 252.5 all-gather.8
  652.4 128.1 all-gather.14
  785.7 295.1 all-gather.10
where the time goes:
time: 1230 us; the launch traced here: 1220 us
  blocking collectives  428 us (35%)
  waiting for transfers between devices  418 us (34%)
  other arithmetic  201 us (16%)
  local copies, waits for them, and re-layouts  110 us (9%)
  matrix products  20.8 us (2%)
  between operations  20.8 us (2%)
  starting transfers between devices  17.2 us (1%)
    all_gather x4, waiting for transfers between devices, carried_in(): gathered = jax.tree.map(lambda a: lax.all_gather(a, axis), part)  403 us
    psum x1, blocking collectives, local(): totals = lax.psum((sum_in, sum_bias, sum_out), ('gx', 'gy'))  262 us
    add x126, other arithmetic, combine(): return (earlier[0] * later[0], later[0] * earlier[1] + later[1])  174 us
    unnamed x1, blocking collectives  149 us
    dynamic_slice x126, local copies, waits for them, and re-layouts, one(): lax.dynamic_index_in_dim(a, source, 0, False)  77 us
  transfers between devices with their start and end apart: 10, of which 8 were waited for; matrix products, arithmetic and copies ran while one was open for 1% of the time, Pallas kernels for 0%

commit v1 on v0

--- a/solution.py
+++ b/solution.py
@@ -169,7 +169,7 @@
     back_y = y_pass(grad_features[0:3], y_table.T)
     back_z = jnp.einsum("ba,kxyb->kxya", z_table, grad_features[3:6], precision=PRECISE)
     grad_velocity = cotangent + smooth_x(back_y + back_z)
-    totals = lax.psum((sum_in, sum_bias, sum_out), ("gx", "gy"))
+    totals = lax.psum(lax.psum((sum_in, sum_bias, sum_out), "gx"), "gy")
     cells = float(x_rows * lax.axis_size("gx") * y_length * z_length)
     return (new_velocity, grad_velocity, totals[0] / cells, totals[1] / cells, totals[2] / cells)
 

time: 1230 us -> 1250 us (1.016)
  the two profiles are of different devices: /device:TPU:2 before, /device:TPU:1 now
where the time goes in v1:
time: 1250 us; the launch traced here: 1240 us
  blocking collectives  469 us (38%)
  waiting for transfers between devices  401 us (32%)
  other arithmetic  197 us (16%)
  local copies, waits for them, and re-layouts  104 us (8%)
  starting transfers between devices  26.6 us (2%)
  matrix products  20.8 us (2%)
  between operations  20.8 us (2%)
    all_gather x4, waiting for transfers between devices, carried_in(): gathered = jax.tree.map(lambda a: lax.all_gather(a, axis), part)  388 us
    psum x2, blocking collectives, local(): totals = lax.psum(lax.psum((sum_in, sum_bias, sum_out), 'gx'), 'gy')  330 us
    add x126, other arithmetic, combine(): return (earlier[0] * later[0], later[0] * earlier[1] + later[1])  169 us
    unnamed x1, blocking collectives  122 us
    dynamic_slice x126, local copies, waits for them, and re-layouts, one(): lax.dynamic_index_in_dim(a, source, 0, False)  71.2 us
  transfers between devices with their start and end apart: 10, of which 7 were waited for; matrix products, arithmetic and copies ran while one was open for 1% of the time, Pallas kernels for 0%

profile of v1, /device:TPU:1, one launch (start us, length us, event | category | flops | bytes accessed | tf_op | source)
XLA Modules:
  0.0 1240.3 jit_solution(9648263071603961455)
XLA Ops:
  8.0 4.0 collective-permute-start
  16.6 3.0 multiply_bitcast_fusion.1
  30.1 122.1 %all-reduce.3 = (f32[64]{0:T(128)S(1)}, f32[64]{0:T(128)S(1)}) all-reduce(f32[64]{0:T(128)S(1)} %dynamic-update-slice.1, f32[64]{0:T(128)S(1)} %dynamic-update-slice), channel_id=1, replica_groups=mesh['gx'=64,'gy'=8] {'gx'}, use_global_device_ids=true, to_apply=%add.1 | all-reduce | flops 128 | bytes 1024
  152.2 6.6 all-gather.13.cloned.1.call-done
  158.9 4.9 fusion.30
  163.8 265.3 %all-gather.9.cloned.1.call-done = f32[192,8,256]{2,1,0:T(8,128)} async-done(((f32[3,8,256]{2,1,0:T(8,128)}), f32[192,8,256]{2,1,0:T(8,128)}) %all-gather.9.cloned.1.call-update) | async-done | bytes 1572880 | tf_op jit(solution)/shard_map/all_gather | solution.py:31
  429.1 124.3 %while.53 = (s32[]{:T(128)}, f32[3,8,256]{2,1,0:T(8,128)S(1)}, s32[]{:T(128)}, f32[64,1,1]{0,2,1:T(1,128)S(1)}, f32[64,3,8,256]{3,2,1,0:T(8,128)}, /*index=5*/s32[]{:T(128)}, s32[]{:T(128)}, s32[]{:T(128)}, s32[]{:T(128)}) while((s32[]{:T(128)}, f32[3,8,256]{2,1,0:T(8,128)S(1)}, s32[]{:T(128)}, f32[64,1,1]{0,2,1:T(1,128)S(1)}, ...), condition=%wide.region_3.4_spmd, body=%wide.region_2.3_spmd.sunk | while | flops 12294 | bytes 73895 | solution.py:40
  429.7 1.4 bitcast_add_fusion.11
  431.7 1.4 bitcast_add_fusion.11
  433.6 1.4 bitcast_add_fusion.11
  435.6 1.4 bitcast_add_fusion.11
  437.6 1.4 bitcast_add_fusion.11
  439.6 1.4 bitcast_add_fusion.11
  441.5 1.4 bitcast_add_fusion.11
  443.5 1.4 bitcast_add_fusion.11
  445.5 1.4 bitcast_add_fusion.11
  447.5 1.4 bitcast_add_fusion.11
  449.4 1.4 bitcast_add_fusion.11
  451.4 1.4 bitcast_add_fusion.11
  453.4 1.4 bitcast_add_fusion.11
  455.3 1.4 bitcast_add_fusion.11
  457.3 1.4 bitcast_add_fusion.11
  459.3 1.4 bitcast_add_fusion.11
  461.3 1.4 bitcast_add_fusion.11
  553.4 2.6 add_bitcast_fusion.6
  556.8 2.4 reshape.250
  559.2 14.2 %all-to-all-start = ((f32[8,1,3072]{2,1,0:T(1,128)}), f32[8,1,3072]{2,1,0:T(1,128)S(1)}, u32[]{:S(2)}, u32[]{:S(2)}) async-start(f32[8,1,3072]{2,1,0:T(1,128)} %reshape.250), calls=%async_computation | async-start | bytes 196608 | tf_op jit(solution)/shard_map/all_to_all | solution.py:119
  573.6 4.8 all-to-all-done
  579.8 1.9 reshape.251
  584.4 4.1 all-to-all-start.1
  588.8 4.6 all-to-all-done.1
  605.6 1.5 copy.85
  607.0 3.2 reshape.254
  610.2 8.2 all_to_all.72
  619.2 3.1 reshape.255
  622.3 2.2 copy.86
  625.6 2.2 convolution_bitcast_fusion
  629.9 9.1 all_to_all.73
  638.9 1.5 reduce.7
  646.4 3.3 collective-permute-done.3
  649.7 3.0 multiply_bitcast_fusion
  656.5 115.7 %all-gather.15.cloned.1.call-done = f32[192,1,8,256]{3,2,1,0:T(8,128)} async-done(((f32[3,1,8,256]{3,2,1,0:T(8,128)}), f32[192,1,8,256]{3,2,1,0:T(8,128)}) %all-gather.15.cloned.1.call-update) | async-done | bytes 1572880 | tf_op jit(solution)/shard_map/all_gather | solution.py:31
  772.2 4.9 fusion.24
  779.4 1.6 convolution_add_fusion.5
  781.0 280.0 %all-reduce.2 = (f32[6,64]{1,0:T(8,128)S(1)}, f32[64]{0:T(128)S(1)}, f32[64,3]{0,1:T(4,128)S(1)}) all-reduce(f32[6,64]{1,0:T(8,128)S(1)} %convolution_add_fusion.5, f32[64]{0:T(128)S(1)} %copy-done.27, f32[64,3]{0,1:T(4,128)S(1)} %convolution_add_fusion.8), channel_id=1, replica_groups=mesh['gx'=64,'gy'=8] {'gx'}, use_global_device_ids=true, to_apply=%region_8.9 | all-reduce | flops 640 | bytes 5120 | tf_op jit(solution)/shard_map/psum | solution.py:172
  1061.0 50.2 %all-reduce.4 = (f32[6,64]{1,0:T(8,128)S(1)}, f32[64]{0:T(128)S(1)}, f32[64,3]{0,1:T(4,128)S(1)}) all-reduce(f32[6,64]{1,0:T(8,128)S(1)} %get-tuple-element.320, f32[64]{0:T(128)S(1)} %get-tuple-element.321, f32[64,3]{0,1:T(4,128)S(1)} %get-tuple-element.322), channel_id=1, replica_groups=mesh['gx'=64,'gy'=8] {'gy'}, use_global_device_ids=true, to_apply=%region_9.10 | all-reduce | flops 640 | bytes 5120 | tf_op jit(solution)/shard_map/psum | solution.py:172
  1115.1 116.1 %while.55 = (s32[]{:T(128)}, f32[3,8,256]{2,1,0:T(8,128)S(1)}, s32[]{:T(128)}, f32[64,1,1]{0,2,1:T(1,128)S(1)}, f32[64,3,8,256]{3,2,1,0:T(8,128)}, /*index=5*/s32[]{:T(128)}, s32[]{:T(128)}, s32[]{:T(128)}, s32[]{:T(128)}) while((s32[]{:T(128)}, f32[3,8,256]{2,1,0:T(8,128)S(1)}, s32[]{:T(128)}, f32[64,1,1]{0,2,1:T(1,128)S(1)}, ...), condition=%wide.region_7.8_spmd, body=%wide.region_6.7_spmd.sunk | while | flops 12294 | bytes 73895 | solution.py:40
  1231.3 1.8 add_bitcast_fusion.2
  (402 shorter events, 263.8 us)
Async XLA Ops:
  7.2 587.9 %copy-start = (f32[6,64]{1,0:T(8,128)S(1)}, f32[6,64]{1,0:T(8,128)}, u32[]{:S(2)}) copy-start(f32[6,64]{1,0:T(8,128)} %param.21) | copy-start | bytes 4612
  7.2 151.7 %all-gather.13.cloned.1.call-start = ((), (), s32[]{:S(2)}) async-start(), calls=%async_computation.6 | async-start | bytes 1597440 | tf_op jit(solution)/shard_map/all_gather | solution.py:31
  8.0 7.7 collective-permute-start
  12.0 4.6 collective-permute-start.1
  19.6 409.5 %all-gather.9.cloned.1.call-start = ((), (), s32[]{:S(2)}) async-start(), calls=%async_computation.4 | async-start | bytes 1597440 | tf_op jit(solution)/shard_map/all_gather | solution.py:31
  158.9 270.2 %copy-start.30 = (f32[64,1,1]{0,2,1:T(1,128)}, f32[64,1,1]{0,2,1:T(1,128)S(1)}, u32[]{:S(2)}) copy-start(f32[64,1,1]{0,2,1:T(1,128)S(1)} %get-tuple-element.637) | copy-start | bytes 772
  553.4 2.6 copy-start.28
  556.0 17.4 %copy-start.13 = (f32[3,4,8,256]{3,2,1,0:T(8,128)S(1)}, f32[3,4,8,256]{3,2,1,0:T(8,128)}, u32[]{:S(2)}) copy-start(f32[3,4,8,256]{3,2,1,0:T(8,128)} %param.20) | copy-start | bytes 294916
  559.2 19.2 %all-to-all-start = ((f32[8,1,3072]{2,1,0:T(1,128)}), f32[8,1,3072]{2,1,0:T(1,128)S(1)}, u32[]{:S(2)}, u32[]{:S(2)}) async-start(f32[8,1,3072]{2,1,0:T(1,128)} %reshape.250), calls=%async_computation | async-start | bytes 196608 | tf_op jit(solution)/shard_map/all_to_all | solution.py:119
  573.5 28.8 %copy-start.19 = (f32[1,3,8,256]{3,1,2,0:T(4,128)}, f32[1,3,8,256]{3,1,2,0:T(4,128)S(1)}, u32[]{:S(2)}) copy-start(f32[1,3,8,256]{3,1,2,0:T(4,128)S(1)} %copy.110) | copy-start | bytes 73732
  573.5 25.4 %copy-start.15 = (f32[1,3,8,256]{3,1,2,0:T(4,128)}, f32[1,3,8,256]{3,1,2,0:T(4,128)S(1)}, u32[]{:S(2)}) copy-start(f32[1,3,8,256]{3,1,2,0:T(4,128)S(1)} %copy.114) | copy-start | bytes 73732
  573.5 24.2 %copy-start.20 = (f32[1,3,8,256]{3,1,2,0:T(4,128)}, f32[1,3,8,256]{3,1,2,0:T(4,128)S(1)}, u32[]{:S(2)}) copy-start(f32[1,3,8,256]{3,1,2,0:T(4,128)S(1)} %copy.112) | copy-start | bytes 73732
  573.6 27.1 %copy-start.17 = (f32[1,3,8,256]{3,1,2,0:T(4,128)}, f32[1,3,8,256]{3,1,2,0:T(4,128)S(1)}, u32[]{:S(2)}) copy-start(f32[1,3,8,256]{3,1,2,0:T(4,128)S(1)} %copy.116) | copy-start | bytes 73732
  579.8 2.6 copy-start.25
  582.3 6.2 copy-start.22
  584.4 9.1 all-to-all-start.1
  588.4 183.7 %all-gather.15.cloned.1.call-start = ((), (), s32[]{:S(2)}) async-start(), calls=%async_computation.7 | async-start | bytes 1597440 | tf_op jit(solution)/shard_map/all_gather | solution.py:31
  594.6 0.7 copy-start.26
  594.8 3.0 copy-start.24
  594.9 2.9 copy-start.11
  594.9 2.2 copy-start.7
  595.0 2.8 copy-start.5
  595.0 2.1 copy-start.9
  601.9 3.6 copy-start.1
  603.6 0.8 copy-start.2
  642.5 11.9 copy-start.21
  642.5 12.4 %copy-start.16 = (f32[1,3,8,256]{3,1,2,0:T(4,128)S(1)}, f32[1,3,8,256]{3,1,2,0:T(4,128)}, u32[]{:S(2)}) copy-start(f32[1,3,8,256]{3,1,2,0:T(4,128)} %copy-done.15) | copy-start | bytes 73732
  642.5 13.5 %copy-start.12 = (f32[1,6,8,256]{3,1,2,0:T(8,128)S(1)}, f32[1,6,8,256]{3,1,2,0:T(8,128)}, u32[]{:S(2)}) copy-start(f32[1,6,8,256]{3,1,2,0:T(8,128)} %copy-done.11) | copy-start | bytes 147460
  643.8 2.6 collective-permute-start.2
  645.1 4.6 collective-permute-start.3
  652.7 462.4 %all-gather.11.cloned.1.call-start = ((), (), s32[]{:S(2)}) async-start(), calls=%async_computation.5 | async-start | bytes 1597440 | tf_op jit(solution)/shard_map/all_gather | solution.py:31
  653.0 2.4 copy-start.18
  653.0 3.0 copy-start.3
  654.3 123.9 %copy-start.8 = (f32[1,6,8,256]{3,1,2,0:T(8,128)S(1)}, f32[1,6,8,256]{3,1,2,0:T(8,128)}, u32[]{:S(2)}) copy-start(f32[1,6,8,256]{3,1,2,0:T(8,128)} %copy-done.7) | copy-start | bytes 147460
  654.9 123.9 %copy-start.10 = (f32[1,6,8,256]{3,1,2,0:T(8,128)S(1)}, f32[1,6,8,256]{3,1,2,0:T(8,128)}, u32[]{:S(2)}) copy-start(f32[1,6,8,256]{3,1,2,0:T(8,128)} %copy-done.9) | copy-start | bytes 147460
  655.4 123.9 %copy-start.6 = (f32[1,6,8,256]{3,1,2,0:T(8,128)S(1)}, f32[1,6,8,256]{3,1,2,0:T(8,128)}, u32[]{:S(2)}) copy-start(f32[1,6,8,256]{3,1,2,0:T(8,128)} %copy-done.5) | copy-start | bytes 147460
  778.3 2.7 copy-start.27
  779.3 335.1 %copy-start.4 = (f32[3,4,8,256]{3,2,1,0:T(8,128)S(1)}, f32[3,4,8,256]{3,2,1,0:T(8,128)}, u32[]{:S(2)}) copy-start(f32[3,4,8,256]{3,2,1,0:T(8,128)} %param.19) | copy-start | bytes 294916
  779.4 335.8 %copy-start.29 = (f32[64,1,1]{0,2,1:T(1,128)S(1)}, f32[64,1,1]{0,2,1:T(1,128)}, u32[]{:S(2)}) copy-start(f32[64,1,1]{0,2,1:T(1,128)} %copy-done.28) | copy-start | bytes 772
  1113.2 118.1 %copy-start.23 = (f32[3,8,256]{2,1,0:T(8,128)S(1)}, f32[3,8,256]{2,1,0:T(8,128)}, u32[]{:S(2)}) copy-start(f32[3,8,256]{2,1,0:T(8,128)} %get-tuple-element.328) | copy-start | bytes 73732
  1113.2 119.9 %copy-start.14 = (f32[3,4,8,256]{3,2,1,0:T(8,128)S(1)}, f32[3,4,8,256]{3,2,1,0:T(8,128)}, u32[]{:S(2)}) copy-start(f32[3,4,8,256]{3,2,1,0:T(8,128)} %param.20) | copy-start | bytes 294916
Sparse Core Ops, SparseCore 0:
  19.8 139.0 all-gather.12
  164.0 265.1 all-gather.8
  652.8 119.2 all-gather.14
  777.2 296.3 all-gather.10
